TPU v7x, 256 devices: a whole 4x4x8 slice. The times are simulated.
256 devices in a mesh: cluster: 8 (over z_hi, core), shard: 32 (over x, z_lo, y).
Axes of the slice: x: 4, y: 4, z: 8 (z_hi: 4, z_lo: 2; z = z_hi * 2 + z_lo), core: 2. Of those that a mesh axis runs over, the one named last changes fastest.
Arguments:
- flow_start: float32 [4096, 256], P(('cluster', 'shard')), may hold values from 0 to 1
- demand: float32 [4096, 256], P(('cluster', 'shard')), may hold values from 0.25 to 2
- utility: float32 [4096, 256], P(('cluster', 'shard')), may hold values from 1 to 16
- path_count: int32 [4096], P(('cluster', 'shard')), may hold values from 1 to 256, as said below
- cluster_size: int32 [8], P('cluster'), may hold values from 1 to 16, as said below
- incidence: float32 [8192, 256, 128], P(('cluster', 'shard')), may hold values from 0 to 1, as said below
- inc_path: int32 [8192], P(('cluster', 'shard')), may hold values from 0 to 511, as said below
- inc_edge: int32 [8192], P(('cluster', 'shard')), may hold values from 0 to 6
- capacity: float32 [1792, 128], P(('cluster', 'shard')), may hold values from 0.25 to 4
- dual_start: float32 [1792, 128], P(('cluster', 'shard')), may hold values from 0 to 7
- partner: int32 [8, 3], P('cluster'), may hold values from 0 to 7, as said below
Outputs:
- flows: float32 [4096, 256], P(('cluster', 'shard'))
- duals: float32 [1792, 128], P(('cluster', 'shard'))
Inputs may be any that keep to these rules, and one draw needn't show every extreme that they name: `path_count`: some path block has 256 live paths. `cluster_size`: some cluster has 16. partner[c, k] = q implies partner[q, k] = c; the partners of a cluster are distinct and differ from it. `incidence`: every entry is 0 or 1. Among the 32 incidence blocks of one device, at most 2 have the same value of inc_path // 16, and on every device some value is taken by exactly 2.
All inputs are finite; a program needn't handle non-finite values.
Results may differ from a plain program's by a relative error of at most 0.0001.
Values sent between devices are 32-bit elements; how exact they have to be, the bound alone decides.
A program may use at most 64 MiB of HBM per device.

v0:
```python
import jax
import jax.numpy as jnp
from jax import lax
from jax.sharding import PartitionSpec as P

ITERS = 3


def body(
    flow_start,
    demand,
    utility,
    path_count,
    cluster_size,
    incidence,
    inc_path,
    inc_edge,
    capacity,
    dual_start,
    partner,
):
    exact_mode = lax.Precision.HIGHEST
    block_count, path_width = flow_start.shape
    inc_count = incidence.shape[0]
    edge_width = incidence.shape[2]
    local_blocks = capacity.shape[0]
    slot_count = partner.shape[1]
    interior = local_blocks - slot_count
    clusters = lax.axis_size("cluster")
    norm_bound = max(
        2, inc_count * inc_count * path_width * edge_width // (1024 * local_blocks * block_count)
    )
    capacity_unit = float(max(1, inc_count * path_width // (160 * local_blocks)))
    step_size = 1.0 / (2.0 * norm_bound)
    block_ids = jnp.arange(block_count, dtype=jnp.int32)
    path_ids = jnp.arange(path_width, dtype=jnp.int32)
    live_mask = (
        (block_ids < cluster_size[0])[:, None] & (path_ids[None, :] < path_count[:, None])
    ).astype(jnp.float32)
    edge_pick = (jnp.arange(local_blocks, dtype=jnp.int32)[:, None] == inc_edge[None, :]).astype(
        jnp.float32
    )
    partner_pick = (jnp.arange(clusters, dtype=jnp.int32)[:, None] == partner[0][None, :]).astype(
        jnp.float32
    )

    def twin_of(border):
        outgoing = jnp.dot(partner_pick, border, precision=exact_mode)
        incoming = lax.all_to_all(outgoing, "cluster", split_axis=0, concat_axis=0, tiled=True)
        return jnp.dot(partner_pick.T, incoming, precision=exact_mode)

    cap_border = capacity[interior:]
    dual_border = dual_start[interior:]
    outgoing = jnp.einsum(
        "ck,mke->cme", partner_pick, jnp.stack([cap_border, dual_border]), precision=exact_mode
    )
    incoming = lax.all_to_all(outgoing, "cluster", split_axis=0, concat_axis=0, tiled=True)
    twins = jnp.einsum("ck,cme->mke", partner_pick, incoming, precision=exact_mode)
    limit = capacity_unit * jnp.concatenate(
        [capacity[:interior], 0.5 * (cap_border + twins[0])], axis=0
    )
    duals = jnp.concatenate([dual_start[:interior], 0.5 * (dual_border + twins[1])], axis=0)

    def load_of_rows(picked):
        terms = jnp.einsum("ipe,ip->ie", incidence, picked, precision=exact_mode)
        own_load = jnp.dot(edge_pick, terms, precision=exact_mode)
        border = own_load[interior:]
        return jnp.concatenate([own_load[:interior], border + twin_of(border)], axis=0)

    def total_load(gathered):
        return load_of_rows(jnp.take(gathered, inc_path, axis=0))

    def settle(load, duals_now):
        split = jnp.minimum(limit, load + duals_now)
        return (split, duals_now + load - split)

    flows = jnp.minimum(jnp.maximum(flow_start, 0.0), demand) * live_mask

    def shared_flows(flows_now):
        return lax.all_gather(flows_now, "shard", axis=0, tiled=True)

    load = total_load(shared_flows(flows))
    split, duals = settle(load, duals)
    for iteration in range(ITERS):
        residual = load - split + duals
        residual_picked = jnp.take(residual, inc_edge, axis=0)
        terms = jnp.einsum("ipe,ie->ip", incidence, residual_picked, precision=exact_mode)
        rows_pick = (
            jnp.arange(block_count * lax.axis_size("shard"), dtype=jnp.int32)[:, None]
            == inc_path[None, :]
        ).astype(jnp.float32)
        gradient = lax.psum_scatter(
            jnp.dot(rows_pick, terms, precision=exact_mode),
            "shard",
            scatter_dimension=0,
            tiled=True,
        )
        flows = (
            jnp.minimum(jnp.maximum(flows - step_size * (gradient - utility), 0.0), demand)
            * live_mask
        )
        load = total_load(shared_flows(flows))
        split, duals = settle(load, duals)
    return (flows, duals)


def solution(mesh):
    return jax.shard_map(
        body,
        mesh=mesh,
        in_specs=(
            P(("cluster", "shard"), None),
            P(("cluster", "shard"), None),
            P(("cluster", "shard"), None),
            P(("cluster", "shard")),
            P("cluster"),
            P(("cluster", "shard"), None, None),
            P(("cluster", "shard")),
            P(("cluster", "shard")),
            P(("cluster", "shard"), None),
            P(("cluster", "shard"), None),
            P("cluster", None),
        ),
        out_specs=(P(("cluster", "shard"), None), P(("cluster", "shard"), None)),
        check_vma=False,
    )
```

profile of v0, /device:TPU:1, one launch (start us, length us, event | category | flops | bytes accessed | tf_op | source)
XLA Modules:
  0.0 920.1 jit_solution(6697938760290475055)
XLA Ops:
  7.2 0.7 compare_and_fusion.1
  7.9 0.7 compare_select_fusion.1
  9.2 0.8 minimum_select_fusion.3
  10.0 71.7 %all_gather.12 = f32[512,256]{1,0:T(8,128)S(1)} all-gather(f32[16,256]{1,0:T(8,128)S(1)} %minimum_select_fusion.3), channel_id=1, replica_groups=mesh['cluster'=8,'shard'=32] {'shard'}, dimensions={0}, use_global_device_ids=true | all-gather | bytes 540672 | tf_op jit(solution)/shard_map/all_gather | solution.py:80
  81.8 0.6 gather_fusion
  82.5 4.4 fusion.18
  87.0 0.9 fusion.39
  87.8 21.9 %all-to-all-start = ((f32[8,1,128]{2,1,0:T(1,128)}), f32[8,1,128]{2,1,0:T(1,128)S(1)}, u32[]{:S(2)}, u32[]{:S(2)}) async-start(f32[8,1,128]{2,1,0:T(1,128)} %bitcast.6), calls=%async_computation | async-start | bytes 8192 | tf_op jit(solution)/shard_map/all_to_all | solution.py:49
  109.8 0.3 fusion.22
  110.1 0.6 copy.20
  110.7 6.0 all-to-all-done
  116.7 3.9 all-to-all-start.1
  120.8 6.9 all-to-all-done.1
  127.6 0.2 convolution_bitcast_fusion
  127.9 0.6 gather_fusion.1
  128.5 5.7 fusion.61
  134.2 1.2 fusion.2
  135.4 128.4 %reduce-scatter.4.cloned.1.call-done = f32[16,256]{1,0:T(8,128)} async-done(((f32[512,256]{1,0:T(8,128)}), f32[16,256]{1,0:T(8,128)}) %reduce-scatter.4.cloned.1.call-update) | async-done | bytes 16400 | tf_op jit(solution)/shard_map/reduce_scatter | solution.py:92
  263.8 0.8 minimum_select_fusion.2
  264.6 65.2 %all_gather.13 = f32[512,256]{1,0:T(8,128)S(1)} all-gather(f32[16,256]{1,0:T(8,128)S(1)} %minimum_select_fusion.2), channel_id=1, replica_groups=mesh['cluster'=8,'shard'=32] {'shard'}, dimensions={0}, use_global_device_ids=true | all-gather | bytes 540672 | tf_op jit(solution)/shard_map/all_gather | solution.py:80
  329.7 0.6 gather_fusion.2
  330.4 4.3 fusion.15
  334.9 0.9 fusion.37
  335.7 46.7 %all-to-all-start.2 = ((f32[8,1,128]{2,1,0:T(1,128)}), f32[8,1,128]{2,1,0:T(1,128)S(1)}, u32[]{:S(2)}, u32[]{:S(2)}) async-start(f32[8,1,128]{2,1,0:T(1,128)} %bitcast.21), calls=%async_computation.3 | async-start | bytes 8192 | tf_op jit(solution)/shard_map/all_to_all | solution.py:49
  382.4 6.9 all-to-all-done.2
  389.6 0.6 gather_fusion.3
  390.2 5.7 fusion.62
  395.9 1.2 fusion.1
  397.1 128.4 %reduce-scatter.6.cloned.1.call-done = f32[16,256]{1,0:T(8,128)} async-done(((f32[512,256]{1,0:T(8,128)}), f32[16,256]{1,0:T(8,128)}) %reduce-scatter.6.cloned.1.call-update) | async-done | bytes 16400 | tf_op jit(solution)/shard_map/reduce_scatter | solution.py:92
  525.5 0.8 minimum_select_fusion.1
  526.2 65.5 %all_gather.14 = f32[512,256]{1,0:T(8,128)S(1)} all-gather(f32[16,256]{1,0:T(8,128)S(1)} %minimum_select_fusion.1), channel_id=1, replica_groups=mesh['cluster'=8,'shard'=32] {'shard'}, dimensions={0}, use_global_device_ids=true | all-gather | bytes 540672 | tf_op jit(solution)/shard_map/all_gather | solution.py:80
  591.7 0.6 gather_fusion.4
  592.4 4.3 fusion.12
  596.8 0.9 fusion.36
  597.7 46.2 %all-to-all-start.3 = ((f32[8,1,128]{2,1,0:T(1,128)}), f32[8,1,128]{2,1,0:T(1,128)S(1)}, u32[]{:S(2)}, u32[]{:S(2)}) async-start(f32[8,1,128]{2,1,0:T(1,128)} %bitcast.30), calls=%async_computation.5 | async-start | bytes 8192 | tf_op jit(solution)/shard_map/all_to_all | solution.py:49
  643.9 6.9 all-to-all-done.3
  651.1 0.6 gather_fusion.5
  651.7 5.7 fusion.63
  657.4 1.2 fusion
  658.6 128.6 %reduce-scatter.8.cloned.1.call-done = f32[16,256]{1,0:T(8,128)} async-done(((f32[512,256]{1,0:T(8,128)}), f32[16,256]{1,0:T(8,128)}) %reduce-scatter.8.cloned.1.call-update) | async-done | bytes 16400 | tf_op jit(solution)/shard_map/reduce_scatter | solution.py:92
  787.2 0.8 minimum_select_fusion
  788.0 65.5 %all_gather.15 = f32[512,256]{1,0:T(8,128)S(1)} all-gather(f32[16,256]{1,0:T(8,128)S(1)} %minimum_select_fusion), channel_id=1, replica_groups=mesh['cluster'=8,'shard'=32] {'shard'}, dimensions={0}, use_global_device_ids=true | all-gather | bytes 540672 | tf_op jit(solution)/shard_map/all_gather | solution.py:80
  853.5 0.6 gather_fusion.6
  854.2 4.3 fusion.9
  858.6 0.9 fusion.35
  859.5 46.3 %all-to-all-start.4 = ((f32[8,1,128]{2,1,0:T(1,128)}), f32[8,1,128]{2,1,0:T(1,128)S(1)}, u32[]{:S(2)}, u32[]{:S(2)}) async-start(f32[8,1,128]{2,1,0:T(1,128)} %bitcast.39), calls=%async_computation.7 | async-start | bytes 8192 | tf_op jit(solution)/shard_map/all_to_all | solution.py:49
  905.8 6.9 all-to-all-done.4
  912.9 0.6 minimum_subtract_fusion
  (57 shorter events, 2.0 us)
Async XLA Ops:
  7.2 79.7 %copy-start.6 = (s32[32]{0:T(128)S(1)}, s32[32]{0:T(128)}, u32[]{:S(2)}) copy-start(s32[32]{0:T(128)} %param.22) | copy-start | bytes 388
  7.2 79.8 %copy-start.9 = (s32[1,3]{1,0:T(1,128)S(1)}, s32[1,3]{1,0:T(1,128)}, u32[]{:S(2)}) copy-start(s32[1,3]{1,0:T(1,128)} %param.25) | copy-start | bytes 40
  7.2 102.6 %copy-start.4 = (f32[7,128]{1,0:T(8,128)S(1)}, f32[7,128]{1,0:T(8,128)}, u32[]{:S(2)}) copy-start(f32[7,128]{1,0:T(8,128)} %param.24) | copy-start | bytes 10756
  7.2 102.6 %copy-start.5 = (f32[7,128]{1,0:T(8,128)S(1)}, f32[7,128]{1,0:T(8,128)}, u32[]{:S(2)}) copy-start(f32[7,128]{1,0:T(8,128)} %param.23) | copy-start | bytes 10756
  82.5 51.7 %copy-start.8 = (s32[32]{0:T(128)S(1)}, s32[32]{0:T(128)}, u32[]{:S(2)}) copy-start(s32[32]{0:T(128)} %param.21) | copy-start | bytes 388
  82.5 181.3 %copy-start = (f32[16,256]{1,0:T(8,128)S(1)}, f32[16,256]{1,0:T(8,128)}, u32[]{:S(2)}) copy-start(f32[16,256]{1,0:T(8,128)} %param.16) | copy-start | bytes 49156
  82.5 181.3 %copy-start.1 = (f32[16,256]{1,0:T(8,128)S(1)}, f32[16,256]{1,0:T(8,128)}, u32[]{:S(2)}) copy-start(f32[16,256]{1,0:T(8,128)} %param.17) | copy-start | bytes 49156
  82.5 181.3 %copy-start.2 = (f32[16,256]{1,0:T(8,128)S(1)}, f32[16,256]{1,0:T(8,128)}, u32[]{:S(2)}) copy-start(f32[16,256]{1,0:T(8,128)} %param.15) | copy-start | bytes 49156
  82.5 181.3 %copy-start.7 = (s32[16]{0:T(128)S(1)}, s32[16]{0:T(128)}, u32[]{:S(2)}) copy-start(s32[16]{0:T(128)} %param.18) | copy-start | bytes 196
  87.8 28.8 %all-to-all-start = ((f32[8,1,128]{2,1,0:T(1,128)}), f32[8,1,128]{2,1,0:T(1,128)S(1)}, u32[]{:S(2)}, u32[]{:S(2)}) async-start(f32[8,1,128]{2,1,0:T(1,128)} %bitcast.6), calls=%async_computation | async-start | bytes 8192 | tf_op jit(solution)/shard_map/all_to_all | solution.py:49
  116.7 11.0 %all-to-all-start.1 = ((f32[8,2,128]{2,1,0:T(2,128)}), f32[8,2,128]{2,1,0:T(2,128)S(1)}, u32[]{:S(2)}, u32[]{:S(2)}) async-start(f32[8,2,128]{2,1,0:T(2,128)} %copy.20), calls=%async_computation.1 | async-start | bytes 16384 | tf_op jit(solution)/shard_map/all_to_all | solution.py:57
  120.6 143.2 %reduce-scatter.4.cloned.1.call-start = ((), (), s32[]{:S(2)}) async-start(), calls=%async_computation.8 | async-start | bytes 540672 | tf_op jit(solution)/shard_map/reduce_scatter | solution.py:92
  335.7 53.6 %all-to-all-start.2 = ((f32[8,1,128]{2,1,0:T(1,128)}), f32[8,1,128]{2,1,0:T(1,128)S(1)}, u32[]{:S(2)}, u32[]{:S(2)}) async-start(f32[8,1,128]{2,1,0:T(1,128)} %bitcast.21), calls=%async_computation.3 | async-start | bytes 8192 | tf_op jit(solution)/shard_map/all_to_all | solution.py:49
  382.4 143.0 %reduce-scatter.6.cloned.1.call-start = ((), (), s32[]{:S(2)}) async-start(), calls=%async_computation.9 | async-start | bytes 540672 | tf_op jit(solution)/shard_map/reduce_scatter | solution.py:92
  597.7 53.1 %all-to-all-start.3 = ((f32[8,1,128]{2,1,0:T(1,128)}), f32[8,1,128]{2,1,0:T(1,128)S(1)}, u32[]{:S(2)}, u32[]{:S(2)}) async-start(f32[8,1,128]{2,1,0:T(1,128)} %bitcast.30), calls=%async_computation.5 | async-start | bytes 8192 | tf_op jit(solution)/shard_map/all_to_all | solution.py:49
  643.9 143.2 %reduce-scatter.8.cloned.1.call-start = ((), (), s32[]{:S(2)}) async-start(), calls=%async_computation.10 | async-start | bytes 540672 | tf_op jit(solution)/shard_map/reduce_scatter | solution.py:92
  788.0 125.6 %copy-start.3 = (f32[16,256]{1,0:T(8,128)}, f32[16,256]{1,0:T(8,128)S(1)}, u32[]{:S(2)}) copy-start(f32[16,256]{1,0:T(8,128)S(1)} %minimum_select_fusion) | copy-start | bytes 49156
  859.5 53.3 %all-to-all-start.4 = ((f32[8,1,128]{2,1,0:T(1,128)}), f32[8,1,128]{2,1,0:T(1,128)S(1)}, u32[]{:S(2)}, u32[]{:S(2)}) async-start(f32[8,1,128]{2,1,0:T(1,128)} %bitcast.39), calls=%async_computation.7 | async-start | bytes 8192 | tf_op jit(solution)/shard_map/all_to_all | solution.py:49
Sparse Core Ops, SparseCore 0:
  135.5 128.1 reduce-scatter.3
  397.2 128.2 reduce-scatter.5
  658.7 128.3 reduce-scatter.7
where the time goes:
time: 921 us; the launch traced here: 920 us
  waiting for transfers between devices  419 us (45%)
  blocking collectives  268 us (29%)
  starting transfers between devices  165 us (18%)
  matrix products  43 us (5%)
  between operations  14.6 us (2%)
    reduce_scatter x3, waiting for transfers between devices, body(): lax.psum_scatter(jnp.dot(rows_pick, terms, precision=exact_mode), 'shard'...  385 us
    all_gather x4, blocking collectives, shared_flows(): return lax.all_gather(flows_now, 'shard', axis=0, tiled=True)  268 us
    all_to_all x4, starting transfers between devices, twin_of(): lax.all_to_all(outgoing, 'cluster', split_axis=0, concat_axis=0, tiled=True)  161 us
    all_to_all x4, waiting for transfers between devices, twin_of(): lax.all_to_all(outgoing, 'cluster', split_axis=0, concat_axis=0, tiled=True)  26.7 us
  transfers between devices with their start and end apart: 8, of which 8 were waited for; matrix products, arithmetic and copies ran while one was open for 0% of the time, Pallas kernels for 0%

commit v1 on v0

--- a/solution.py
+++ b/solution.py
@@ -77,7 +77,9 @@
     flows = jnp.minimum(jnp.maximum(flow_start, 0.0), demand) * live_mask
 
     def shared_flows(flows_now):
-        return lax.all_gather(flows_now, "shard", axis=0, tiled=True)
+        return jnp.concatenate(
+            lax.all_to_all(jnp.stack([flows_now] * lax.axis_size("shard")), "shard", 0, 0), axis=0
+        )
 
     load = total_load(shared_flows(flows))
     split, duals = settle(load, duals)

time: 921 us -> 664 us (0.72)
  blocking collectives: 268 us -> 35.9 us
  starting transfers between devices: 165 us -> 125 us
  waiting for transfers between devices: 419 us -> 429 us
    all_gather x4 -> x0, blocking collectives: 268 us -> none  [shared_flows(): return lax.all_gather(flows_now, 'shard', axis=0, tiled=True)]
    all_to_all x4, starting transfers between devices: 161 us -> 107 us  [twin_of(): lax.all_to_all(outgoing, 'cluster', split_axis=0, concat_axis=0, tiled=True)]
    all_to_all x0 -> x3, blocking collectives: none -> 35.9 us  [shared_flows(): lax.all_to_all(jnp.stack([flows_now] * lax.axis_size('shard')), 'shard',...]
  transfers between devices with their start and end apart: 8 -> 9, of which waited for: 8 -> 9; matrix products, arithmetic and copies ran while one was open for 0% -> 1% of each run, Pallas kernels for 0% -> 0%
where the time goes in v1:
time: 664 us; the launch traced here: 663 us
  waiting for transfers between devices  429 us (65%)
  starting transfers between devices  125 us (19%)
  matrix products  44.3 us (7%)
  blocking collectives  35.9 us (5%)
  between operations  14.6 us (2%)
  local copies, waits for them, and re-layouts  7.93 us (1%)
  other arithmetic  7.06 us (1%)
    reduce_scatter x3, waiting for transfers between devices, body(): lax.psum_scatter(jnp.dot(rows_pick, terms, precision=exact_mode), 'shard'...  391 us
    all_to_all x4, starting transfers between devices, twin_of(): lax.all_to_all(outgoing, 'cluster', split_axis=0, concat_axis=0, tiled=True)  107 us
    all_to_all x3, blocking collectives, shared_flows(): lax.all_to_all(jnp.stack([flows_now] * lax.axis_size('shard')), 'shard',...  35.9 us
    all_to_all x4, waiting for transfers between devices, twin_of(): lax.all_to_all(outgoing, 'cluster', split_axis=0, concat_axis=0, tiled=True)  27.6 us
    dot_general x4, matrix products, load_of_rows(): terms = jnp.einsum('ipe,ip->ie', incidence, picked, precision=exact_mode)  17.3 us
    dot_general x3, matrix products, body(): jnp.einsum('ipe,ie->ip', incidence, residual_picked, precision=exact_mode)  17 us
  transfers between devices with their start and end apart: 9, of which 9 were waited for; matrix products, arithmetic and copies ran while one was open for 1% of the time, Pallas kernels for 0%

profile of v1, /device:TPU:1, one launch (start us, length us, event | category | flops | bytes accessed | tf_op | source)
XLA Modules:
  0.0 663.3 jit_solution(7454245585294808188)
XLA Ops:
  7.2 0.7 slice_bitcast_fusion.2
  7.9 0.9 fusion.22
  8.8 0.6 copy.20
  9.5 10.0 %all-to-all-start.2 = ((f32[8,2,128]{2,1,0:T(2,128)}), f32[8,2,128]{2,1,0:T(2,128)S(1)}, u32[]{:S(2)}, u32[]{:S(2)}) async-start(f32[8,2,128]{2,1,0:T(2,128)} %copy.20), calls=%async_computation.2 | async-start | bytes 16384 | tf_op jit(solution)/shard_map/all_to_all | solution.py:57
  20.1 0.8 minimum_select_fusion.3
  20.9 0.7 compare_select_fusion.1
  21.6 4.9 all-to-all-done.2
  26.5 0.9 stack.14
  27.3 7.5 %all-to-all-start = ((f32[32,16,256]{2,1,0:T(8,128)}), f32[32,16,256]{2,1,0:T(8,128)S(1)}, u32[]{:S(2)}, u32[]{:S(2)}) async-start(f32[32,16,256]{2,1,0:T(8,128)} %stack.14), calls=%async_computation | async-start | bytes 1048576 | tf_op jit(solution)/shard_map/all_to_all | solution.py:81
  34.8 0.7 slice.44
  35.5 0.7 slice.48
  36.2 0.7 compare_select_fusion
  36.9 0.7 compare_and_fusion.1
  37.5 0.7 compare_and_fusion
  38.2 0.8 convolution_bitcast_fusion
  39.0 5.6 all-to-all-done
  45.4 4.4 fusion.18
  49.8 0.9 fusion.39
  50.7 5.9 all-to-all-start.1
  56.6 6.9 %all-to-all-done.1 = f32[8,1,128]{2,1,0:T(1,128)S(1)} async-done(((f32[8,1,128]{2,1,0:T(1,128)}), f32[8,1,128]{2,1,0:T(1,128)S(1)}, u32[]{:S(2)}, u32[]{:S(2)}) %all-to-all-start.1) | async-done | bytes 4128 | tf_op jit(solution)/shard_map/all_to_all | solution.py:49
  64.4 5.7 fusion.61
  70.0 1.2 fusion.2
  71.2 130.2 %reduce-scatter.4.cloned.1.call-done = f32[16,256]{1,0:T(8,128)} async-done(((f32[512,256]{1,0:T(8,128)}), f32[16,256]{1,0:T(8,128)}) %reduce-scatter.4.cloned.1.call-update) | async-done | bytes 16400 | tf_op jit(solution)/shard_map/reduce_scatter | solution.py:94
  201.5 0.8 minimum_select_fusion.2
  202.3 12.0 %all_to_all.73 = f32[32,16,256]{2,1,0:T(8,128)S(1)} all-to-all(f32[32,16,256]{2,1,0:T(8,128)S(1)} %stack.18), channel_id=1, replica_groups=mesh['cluster'=8,'shard'=32] {'shard'}, dimensions={0} | all-to-all | bytes 1048576 | tf_op jit(solution)/shard_map/all_to_all | solution.py:81
  215.0 4.3 fusion.15
  219.4 0.9 fusion.37
  220.3 33.8 %all-to-all-start.4 = ((f32[8,1,128]{2,1,0:T(1,128)}), f32[8,1,128]{2,1,0:T(1,128)S(1)}, u32[]{:S(2)}, u32[]{:S(2)}) async-start(f32[8,1,128]{2,1,0:T(1,128)} %bitcast.23), calls=%async_computation.5 | async-start | bytes 8192 | tf_op jit(solution)/shard_map/all_to_all | solution.py:49
  254.1 6.9 %all-to-all-done.4 = f32[8,1,128]{2,1,0:T(1,128)S(1)} async-done(((f32[8,1,128]{2,1,0:T(1,128)}), f32[8,1,128]{2,1,0:T(1,128)S(1)}, u32[]{:S(2)}, u32[]{:S(2)}) %all-to-all-start.4) | async-done | bytes 4128 | tf_op jit(solution)/shard_map/all_to_all | solution.py:49
  261.9 5.7 fusion.62
  267.5 1.2 fusion.1
  268.8 130.2 %reduce-scatter.6.cloned.1.call-done = f32[16,256]{1,0:T(8,128)} async-done(((f32[512,256]{1,0:T(8,128)}), f32[16,256]{1,0:T(8,128)}) %reduce-scatter.6.cloned.1.call-update) | async-done | bytes 16400 | tf_op jit(solution)/shard_map/reduce_scatter | solution.py:94
  398.9 0.8 minimum_select_fusion.1
  399.8 12.0 %all_to_all.74 = f32[32,16,256]{2,1,0:T(8,128)S(1)} all-to-all(f32[32,16,256]{2,1,0:T(8,128)S(1)} %stack.19), channel_id=1, replica_groups=mesh['cluster'=8,'shard'=32] {'shard'}, dimensions={0} | all-to-all | bytes 1048576 | tf_op jit(solution)/shard_map/all_to_all | solution.py:81
  412.4 4.3 fusion.12
  416.9 0.9 fusion.36
  417.7 33.9 %all-to-all-start.6 = ((f32[8,1,128]{2,1,0:T(1,128)}), f32[8,1,128]{2,1,0:T(1,128)S(1)}, u32[]{:S(2)}, u32[]{:S(2)}) async-start(f32[8,1,128]{2,1,0:T(1,128)} %bitcast.33), calls=%async_computation.8 | async-start | bytes 8192 | tf_op jit(solution)/shard_map/all_to_all | solution.py:49
  451.6 6.9 %all-to-all-done.6 = f32[8,1,128]{2,1,0:T(1,128)S(1)} async-done(((f32[8,1,128]{2,1,0:T(1,128)}), f32[8,1,128]{2,1,0:T(1,128)S(1)}, u32[]{:S(2)}, u32[]{:S(2)}) %all-to-all-start.6) | async-done | bytes 4128 | tf_op jit(solution)/shard_map/all_to_all | solution.py:49
  459.4 5.7 fusion.63
  465.0 1.2 fusion
  466.2 130.2 %reduce-scatter.8.cloned.1.call-done = f32[16,256]{1,0:T(8,128)} async-done(((f32[512,256]{1,0:T(8,128)}), f32[16,256]{1,0:T(8,128)}) %reduce-scatter.8.cloned.1.call-update) | async-done | bytes 16400 | tf_op jit(solution)/shard_map/reduce_scatter | solution.py:94
  596.4 0.8 minimum_select_fusion
  597.3 12.0 %all_to_all.75 = f32[32,16,256]{2,1,0:T(8,128)S(1)} all-to-all(f32[32,16,256]{2,1,0:T(8,128)S(1)} %stack.20), channel_id=1, replica_groups=mesh['cluster'=8,'shard'=32] {'shard'}, dimensions={0} | all-to-all | bytes 1048576 | tf_op jit(solution)/shard_map/all_to_all | solution.py:81
  609.9 4.3 fusion.9
  614.4 0.9 fusion.35
  615.2 33.8 %all-to-all-start.8 = ((f32[8,1,128]{2,1,0:T(1,128)}), f32[8,1,128]{2,1,0:T(1,128)S(1)}, u32[]{:S(2)}, u32[]{:S(2)}) async-start(f32[8,1,128]{2,1,0:T(1,128)} %bitcast.43), calls=%async_computation.11 | async-start | bytes 8192 | tf_op jit(solution)/shard_map/all_to_all | solution.py:49
  649.1 6.9 %all-to-all-done.8 = f32[8,1,128]{2,1,0:T(1,128)S(1)} async-done(((f32[8,1,128]{2,1,0:T(1,128)}), f32[8,1,128]{2,1,0:T(1,128)S(1)}, u32[]{:S(2)}, u32[]{:S(2)}) %all-to-all-start.8) | async-done | bytes 4128 | tf_op jit(solution)/shard_map/all_to_all | solution.py:49
  656.2 0.6 minimum_subtract_fusion
  (62 shorter events, 6.2 us)
Async XLA Ops:
  7.2 49.4 %copy-start.4 = (f32[7,128]{1,0:T(8,128)S(1)}, f32[7,128]{1,0:T(8,128)}, u32[]{:S(2)}) copy-start(f32[7,128]{1,0:T(8,128)} %param.24) | copy-start | bytes 10756
  7.2 49.4 %copy-start.5 = (f32[7,128]{1,0:T(8,128)S(1)}, f32[7,128]{1,0:T(8,128)}, u32[]{:S(2)}) copy-start(f32[7,128]{1,0:T(8,128)} %param.23) | copy-start | bytes 10756
  7.2 42.7 %copy-start.9 = (s32[1,3]{1,0:T(1,128)S(1)}, s32[1,3]{1,0:T(1,128)}, u32[]{:S(2)}) copy-start(s32[1,3]{1,0:T(1,128)} %param.25) | copy-start | bytes 40
  7.2 42.5 %copy-start.6 = (s32[32]{0:T(128)S(1)}, s32[32]{0:T(128)}, u32[]{:S(2)}) copy-start(s32[32]{0:T(128)} %param.22) | copy-start | bytes 388
  9.5 17.0 %all-to-all-start.2 = ((f32[8,2,128]{2,1,0:T(2,128)}), f32[8,2,128]{2,1,0:T(2,128)S(1)}, u32[]{:S(2)}, u32[]{:S(2)}) async-start(f32[8,2,128]{2,1,0:T(2,128)} %copy.20), calls=%async_computation.2 | async-start | bytes 16384 | tf_op jit(solution)/shard_map/all_to_all | solution.py:57
  27.3 17.3 %all-to-all-start = ((f32[32,16,256]{2,1,0:T(8,128)}), f32[32,16,256]{2,1,0:T(8,128)S(1)}, u32[]{:S(2)}, u32[]{:S(2)}) async-start(f32[32,16,256]{2,1,0:T(8,128)} %stack.14), calls=%async_computation | async-start | bytes 1048576 | tf_op jit(solution)/shard_map/all_to_all | solution.py:81
  45.3 24.7 %copy-start.8 = (s32[32]{0:T(128)S(1)}, s32[32]{0:T(128)}, u32[]{:S(2)}) copy-start(s32[32]{0:T(128)} %param.21) | copy-start | bytes 388
  45.3 156.1 %copy-start = (f32[16,256]{1,0:T(8,128)S(1)}, f32[16,256]{1,0:T(8,128)}, u32[]{:S(2)}) copy-start(f32[16,256]{1,0:T(8,128)} %param.16) | copy-start | bytes 49156
  45.3 156.1 %copy-start.1 = (f32[16,256]{1,0:T(8,128)S(1)}, f32[16,256]{1,0:T(8,128)}, u32[]{:S(2)}) copy-start(f32[16,256]{1,0:T(8,128)} %param.17) | copy-start | bytes 49156
  45.3 156.1 %copy-start.2 = (f32[16,256]{1,0:T(8,128)S(1)}, f32[16,256]{1,0:T(8,128)}, u32[]{:S(2)}) copy-start(f32[16,256]{1,0:T(8,128)} %param.15) | copy-start | bytes 49156
  45.3 156.1 %copy-start.7 = (s32[16]{0:T(128)S(1)}, s32[16]{0:T(128)}, u32[]{:S(2)}) copy-start(s32[16]{0:T(128)} %param.18) | copy-start | bytes 196
  50.7 12.8 %all-to-all-start.1 = ((f32[8,1,128]{2,1,0:T(1,128)}), f32[8,1,128]{2,1,0:T(1,128)S(1)}, u32[]{:S(2)}, u32[]{:S(2)}) async-start(f32[8,1,128]{2,1,0:T(1,128)} %bitcast.7), calls=%async_computation.1 | async-start | bytes 8192 | tf_op jit(solution)/shard_map/all_to_all | solution.py:49
  56.6 144.9 %reduce-scatter.4.cloned.1.call-start = ((), (), s32[]{:S(2)}) async-start(), calls=%async_computation.12 | async-start | bytes 540672 | tf_op jit(solution)/shard_map/reduce_scatter | solution.py:94
  220.3 40.7 %all-to-all-start.4 = ((f32[8,1,128]{2,1,0:T(1,128)}), f32[8,1,128]{2,1,0:T(1,128)S(1)}, u32[]{:S(2)}, u32[]{:S(2)}) async-start(f32[8,1,128]{2,1,0:T(1,128)} %bitcast.23), calls=%async_computation.5 | async-start | bytes 8192 | tf_op jit(solution)/shard_map/all_to_all | solution.py:49
  254.1 144.8 %reduce-scatter.6.cloned.1.call-start = ((), (), s32[]{:S(2)}) async-start(), calls=%async_computation.13 | async-start | bytes 540672 | tf_op jit(solution)/shard_map/reduce_scatter | solution.py:94
  417.7 40.8 %all-to-all-start.6 = ((f32[8,1,128]{2,1,0:T(1,128)}), f32[8,1,128]{2,1,0:T(1,128)S(1)}, u32[]{:S(2)}, u32[]{:S(2)}) async-start(f32[8,1,128]{2,1,0:T(1,128)} %bitcast.33), calls=%async_computation.8 | async-start | bytes 8192 | tf_op jit(solution)/shard_map/all_to_all | solution.py:49
  451.6 144.8 %reduce-scatter.8.cloned.1.call-start = ((), (), s32[]{:S(2)}) async-start(), calls=%async_computation.14 | async-start | bytes 540672 | tf_op jit(solution)/shard_map/reduce_scatter | solution.py:94
  597.2 59.6 %copy-start.3 = (f32[16,256]{1,0:T(8,128)}, f32[16,256]{1,0:T(8,128)S(1)}, u32[]{:S(2)}) copy-start(f32[16,256]{1,0:T(8,128)S(1)} %minimum_select_fusion) | copy-start | bytes 49156
  615.2 40.7 %all-to-all-start.8 = ((f32[8,1,128]{2,1,0:T(1,128)}), f32[8,1,128]{2,1,0:T(1,128)S(1)}, u32[]{:S(2)}, u32[]{:S(2)}) async-start(f32[8,1,128]{2,1,0:T(1,128)} %bitcast.43), calls=%async_computation.11 | async-start | bytes 8192 | tf_op jit(solution)/shard_map/all_to_all | solution.py:49
Sparse Core Ops, SparseCore 0:
  71.4 130.0 reduce-scatter.3
  268.9 129.9 reduce-scatter.5
  466.4 130.0 reduce-scatter.7
